TPU v7x, 32 devices: a whole 2x2x4 slice. The times are simulated.
32 devices in a mesh: sup: 16 (over z, y, x), cls: 2 (over core).
Axes of the slice: x: 2, y: 2, z: 4, core: 2. Of those that a mesh axis runs over, the one named last changes fastest.
Arguments:
- support_feats: bfloat16 [512, 8192], P('sup', 'cls'), may hold values from -6 to 6
- target_feats: bfloat16 [128, 8192], P('sup', 'cls'), may hold values from -6 to 6
- scales: bfloat16 [512], replicated, may hold values from 0.5 to 2
- soft_labels: float32 [512, 5376], P('sup', 'cls'), may hold values from -6 to 6
- target_labels: int32 [128], P('sup'), may hold values from 0 to 5375
Outputs:
- predictions: bfloat16 [128, 5376], P('sup', 'cls')
- hypergrad: float32 [512, 5376], P('sup', 'cls')
All inputs are finite; a program needn't handle non-finite values.
Results may differ from a plain program's by a relative error of at most 0.017.
Values may be sent and summed in bfloat16 or wider, within the bound.
No kernel may reach another device: no remote copies, remote signals or barrier semaphores. Data moves between devices by JAX's collectives and lax.ppermute only.
A program may use at most 64 MiB of HBM per device.

v0:
```python
import jax
import jax.numpy as jnp
from jax import lax
from jax.sharding import PartitionSpec as P

F = 8192
ITERS = 2
RIDGE = 0.05
LABEL_SCALE = 16.0


def conjugate(rhs, kernel):
    result = jnp.zeros_like(rhs)
    resid = rhs
    direction = rhs
    norm_now = jnp.sum(resid * resid, axis=0)
    for step in range(ITERS):
        image = jnp.dot(kernel, direction.astype(jnp.bfloat16), preferred_element_type=jnp.float32)
        curve = jnp.sum(direction * image, axis=0)
        step_size = norm_now / curve
        result = result + step_size * direction
        resid = resid - step_size * image
        norm_next = jnp.sum(resid * resid, axis=0)
        direction = resid + norm_next / norm_now * direction
        norm_now = norm_next
    return result


def local(support_feats, target_feats, scales, soft_labels, target_labels):
    own_support = support_feats.shape[0]
    own_targets = target_feats.shape[0]
    class_count = soft_labels.shape[1]
    sup_count = lax.axis_size("sup")
    support_total = own_support * sup_count
    block_rows = own_targets + own_support
    scale_vec = scales.astype(jnp.float32)
    sup_index = lax.axis_index("sup")
    support_first = sup_index * own_support
    local_rows = jnp.concatenate([target_feats, support_feats], axis=0)
    partial_gram = lax.dot_general(
        local_rows,
        lax.all_gather(support_feats, "sup", axis=0, tiled=True),
        (((1,), (1,)), ((), ())),
        preferred_element_type=jnp.float32,
    )
    own_scales = lax.dynamic_slice_in_dim(scale_vec, support_first, own_support)
    factor_all = jnp.concatenate([jnp.ones((own_targets,), jnp.float32), own_scales])
    share = lax.psum_scatter(partial_gram, "cls", scatter_dimension=0, tiled=True)
    first_row = lax.axis_index("cls") * share.shape[0]
    count = share.shape[0]
    rows = first_row + lax.iota(jnp.int32, count)
    factor = lax.dynamic_slice_in_dim(factor_all, first_row, count)
    support_index = support_first + rows - own_targets
    on_diag = (lax.iota(jnp.int32, support_total)[None, :] == support_index[:, None]) & (
        rows >= own_targets
    )[:, None]
    scaled = share * (factor[:, None] * scale_vec[None, :]) / F
    finished = (scaled + jnp.where(on_diag, RIDGE, 0.0)).astype(jnp.bfloat16)
    kernels = lax.all_gather(finished, ("sup", "cls"), axis=0, tiled=True)
    blocks = kernels.reshape(sup_count, block_rows, support_total)
    cross_kernel = blocks[:, :own_targets].reshape(sup_count * own_targets, support_total)
    support_kernel = blocks[:, own_targets:].reshape(support_total, support_total)
    label_cols = lax.all_to_all(soft_labels, "sup", split_axis=1, concat_axis=0, tiled=True)
    col_width = label_cols.shape[1]
    labels_all = lax.all_gather(target_labels, "sup", axis=0, tiled=True)
    columns = (
        lax.axis_index("cls") * class_count + sup_index * col_width + lax.iota(jnp.int32, col_width)
    )
    alpha = conjugate(label_cols, support_kernel)
    predicted = jnp.dot(
        cross_kernel, alpha.astype(jnp.bfloat16), preferred_element_type=jnp.float32
    )
    onehot = (labels_all[:, None] == columns[None, :]).astype(jnp.float32)
    misfit = (predicted - LABEL_SCALE * onehot).astype(jnp.bfloat16)
    rhs = lax.dot_general(
        cross_kernel, misfit, (((0,), (0,)), ((), ())), preferred_element_type=jnp.float32
    )
    hyper_cols = conjugate(rhs, support_kernel)
    predictions = lax.all_to_all(
        predicted.astype(jnp.bfloat16), "sup", split_axis=0, concat_axis=1, tiled=True
    )
    hypergrad = lax.all_to_all(hyper_cols, "sup", split_axis=0, concat_axis=1, tiled=True)
    return (predictions, hypergrad)


def solution(mesh):
    in_specs = (P("sup", "cls"), P("sup", "cls"), P(), P("sup", "cls"), P("sup"))
    out_specs = (P("sup", "cls"), P("sup", "cls"))
    return jax.shard_map(local, mesh=mesh, in_specs=in_specs, out_specs=out_specs, check_vma=False)
```

profile of v0, /device:TPU:0, one launch (start us, length us, event | category | flops | bytes accessed | tf_op | source)
XLA Modules:
  0.0 184.7 jit_solution(661950115012459254)
XLA Ops:
  7.2 0.0 copy-start
  7.2 0.0 all-gather.3.cloned.1.call-start
  7.2 0.7 all-gather.3.cloned.1.call-update
  7.9 1.7 all_to_all.42
  9.6 1.1 copy.26
  10.7 8.3 %all-to-all-start = ((f32[32,16,168]{2,0,1:T(8,128)}), f32[32,16,168]{2,0,1:T(8,128)S(1)}, u32[]{:S(2)}, u32[]{:S(2)}) async-start(f32[32,16,168]{2,0,1:T(8,128)} %copy.26), calls=%async_computation | async-start | bytes 1048576 | tf_op jit(solution)/shard_map/all_to_all | solution.py:63
  19.1 0.7 convert_element_type.31
  19.8 0.8 dynamic_slice.6
  20.5 1.2 dynamic-slice.5
  22.4 1.2 dynamic-slice
  24.3 0.9 dynamic-update-slice
  25.2 14.8 %all-reduce.1 = s32[128]{0:T(128)S(1)} all-reduce(s32[128]{0:T(128)S(1)} %dynamic-update-slice), channel_id=1, replica_groups=mesh['sup'=16,'cls'=2] {'sup'}, use_global_device_ids=true, to_apply=%add.1 | all-reduce | flops 128 | bytes 1024
  40.0 0.1 pad_dynamic-slice_fusion
  40.1 0.0 all-to-all-done
  40.1 52.1 %all-gather.3.cloned.1.call-done = bf16[512,4096]{1,0:T(8,128)(2,1)} async-done(((bf16[32,4096]{1,0:T(8,128)(2,1)}), bf16[512,4096]{1,0:T(8,128)(2,1)}) %all-gather.3.cloned.1.call-update) | async-done | bytes 4194320 | tf_op jit(solution)/shard_map/all_gather | solution.py:42
  92.2 0.0 copy-done
  92.2 3.6 %fusion.4 = f32[40,512]{1,0:T(8,128)S(1)} fusion(bf16[512,4096]{1,0:T(8,128)(2,1)} %all-gather.3.cloned.1.call-done, bf16[32,4096]{1,0:T(8,128)(2,1)S(1)} %copy-done, bf16[8,4096]{1,0:T(8,128)(2,1)} %param.6), kind=kOutput, calls=%fused_computation.18 | convolution fusion | flops 168427520 | bytes 4603904 | tf_op jit(solution)/shard_map/dot_general | solution.py:40
  95.8 2.9 %fusion = f32[24,512]{1,0:T(8,128)S(1)} fusion(f32[40,512]{1,0:T(8,128)S(1)} %fusion.4), kind=kCustom, calls=%all-reduce-scatter | all-reduce-scatter fusion | flops 24577 | bytes 131584
  98.8 2.3 %collective-permute-start = (f32[4,512]{1,0:T(4,128)S(1)}, f32[4,512]{1,0:T(4,128)S(1)}, u32[]{:S(2)}, u32[]{:S(2)}) collective-permute-start(f32[4,512]{1,0:T(4,128)S(1)} %slice.10), channel_id=1, source_target_pairs={{0,1},{2,3},{4,5},{6,7},{8,9},{10,11},{12,13},{14,15},{16,17},{18,... | collective-permute-start | bytes 24584
  101.0 0.1 fusion.3
  101.1 0.2 copy.27
  101.3 0.5 collective-permute-done
  101.8 0.1 concatenate.8
  102.0 0.1 fusion.29
  102.1 41.4 %all-gather = bf16[32,20,512]{2,1,0:T(8,128)(2,1)S(1)} all-gather(bf16[1,20,512]{2,1,0:T(8,128)(2,1)S(1)} %fusion.29), channel_id=1, replica_groups=mesh['sup'=16,'cls'=2] {'sup','cls'}, dimensions={0}, use_global_device_ids=true | all-gather | bytes 675840 | tf_op jit(solution)/shard_map/all_gather | solution.py:59
  143.4 0.1 reshape.69
  143.6 0.4 multiply_reduce_fusion.4
  144.1 0.2 multiply_reduce_fusion.3
  144.3 0.5 fusion.1
  144.8 0.3 fusion.34
  145.1 0.2 fusion.20
  145.3 0.5 multiply_reduce_fusion.1
  145.8 0.2 multiply_reduce_fusion
  146.0 0.5 fusion.2
  146.5 0.7 copy.31
  147.2 3.5 %all-to-all-start.1 = ((bf16[16,8,168]{2,1,0:T(8,128)(2,1)}), bf16[16,8,168]{2,1,0:T(8,128)(2,1)S(1)}, u32[]{:S(2)}, u32[]{:S(2)}) async-start(bf16[16,8,168]{2,1,0:T(8,128)(2,1)} %bitcast.7), calls=%async_computation.1 | async-start | bytes 131072 | tf_op jit(solution)/shard_map/all_to_all | solution.py:79
  150.8 0.2 multiply_add_fusion
  150.9 1.0 copy.33
  151.9 6.3 %all-to-all-done.1 = bf16[16,8,168]{2,1,0:T(8,128)(2,1)S(1)} async-done(((bf16[16,8,168]{2,1,0:T(8,128)(2,1)}), bf16[16,8,168]{2,1,0:T(8,128)(2,1)S(1)}, u32[]{:S(2)}, u32[]{:S(2)}) %all-to-all-start.1) | async-done | bytes 43040 | tf_op jit(solution)/shard_map/all_to_all | solution.py:79
  158.3 3.6 %all-to-all-start.2 = ((f32[16,32,168]{2,1,0:T(8,128)}), f32[16,32,168]{2,1,0:T(8,128)S(1)}, u32[]{:S(2)}, u32[]{:S(2)}) async-start(f32[16,32,168]{2,1,0:T(8,128)} %bitcast.10), calls=%async_computation.2 | async-start | bytes 1048576 | tf_op jit(solution)/shard_map/all_to_all | solution.py:82
  161.9 0.8 all_to_all.49
  162.6 13.9 %all-to-all-done.2 = f32[16,32,168]{2,1,0:T(8,128)S(1)} async-done(((f32[16,32,168]{2,1,0:T(8,128)}), f32[16,32,168]{2,1,0:T(8,128)S(1)}, u32[]{:S(2)}, u32[]{:S(2)}) %all-to-all-start.2) | async-done | bytes 344096 | tf_op jit(solution)/shard_map/all_to_all | solution.py:82
  176.6 0.3 copy.34
  176.9 1.0 all_to_all.53
  (14 shorter events, 0.2 us)
Async XLA Ops:
  7.2 85.1 %copy-start = (bf16[32,4096]{1,0:T(8,128)(2,1)S(1)}, bf16[32,4096]{1,0:T(8,128)(2,1)}, u32[]{:S(2)}) copy-start(bf16[32,4096]{1,0:T(8,128)(2,1)} %param.5) | copy-start | bytes 786436
  7.2 85.1 %all-gather.3.cloned.1.call-start = ((), (), s32[]{:S(2)}) async-start(), calls=%async_computation.3 | async-start | bytes 4456448 | tf_op jit(solution)/shard_map/all_gather | solution.py:42
  10.7 29.4 %all-to-all-start = ((f32[32,16,168]{2,0,1:T(8,128)}), f32[32,16,168]{2,0,1:T(8,128)S(1)}, u32[]{:S(2)}, u32[]{:S(2)}) async-start(f32[32,16,168]{2,0,1:T(8,128)} %copy.26), calls=%async_computation | async-start | bytes 1048576 | tf_op jit(solution)/shard_map/all_to_all | solution.py:63
  98.8 3.1 %collective-permute-start = (f32[4,512]{1,0:T(4,128)S(1)}, f32[4,512]{1,0:T(4,128)S(1)}, u32[]{:S(2)}, u32[]{:S(2)}) collective-permute-start(f32[4,512]{1,0:T(4,128)S(1)} %slice.10), channel_id=1, source_target_pairs={{0,1},{2,3},{4,5},{6,7},{8,9},{10,11},{12,13},{14,15},{16,17},{18,... | collective-permute-start | bytes 24584
  147.2 11.0 %all-to-all-start.1 = ((bf16[16,8,168]{2,1,0:T(8,128)(2,1)}), bf16[16,8,168]{2,1,0:T(8,128)(2,1)S(1)}, u32[]{:S(2)}, u32[]{:S(2)}) async-start(bf16[16,8,168]{2,1,0:T(8,128)(2,1)} %bitcast.7), calls=%async_computation.1 | async-start | bytes 131072 | tf_op jit(solution)/shard_map/all_to_all | solution.py:79
  158.3 18.3 %all-to-all-start.2 = ((f32[16,32,168]{2,1,0:T(8,128)}), f32[16,32,168]{2,1,0:T(8,128)S(1)}, u32[]{:S(2)}, u32[]{:S(2)}) async-start(f32[16,32,168]{2,1,0:T(8,128)} %bitcast.10), calls=%async_computation.2 | async-start | bytes 1048576 | tf_op jit(solution)/shard_map/all_to_all | solution.py:82
Sparse Core Ops, SparseCore 0:
  10.7 81.4 all-gather.2
where the time goes:
time: 185 us
  waiting for transfers between devices  73.6 us (40%)
  blocking collectives  59.1 us (32%)
  starting transfers between devices  17.7 us (10%)
  between operations  15.5 us (8%)
  local copies, waits for them, and re-layouts  11.3 us (6%)
  matrix products  5.96 us (3%)
    all_gather x1, waiting for transfers between devices, local(): lax.all_gather(support_feats, 'sup', axis=0, tiled=True)  52.1 us
    all_gather x1, blocking collectives, local(): kernels = lax.all_gather(finished, ('sup', 'cls'), axis=0, tiled=True)  41.4 us
    unnamed x2, blocking collectives  17.7 us
    all_to_all x1, waiting for transfers between devices, local(): lax.all_to_all(hyper_cols, 'sup', split_axis=0, concat_axis=1, tiled=True)  13.9 us
    all_to_all x1, starting transfers between devices, local(): lax.all_to_all(soft_labels, 'sup', split_axis=1, concat_axis=0, tiled=True)  8.34 us
    all_to_all x1, waiting for transfers between devices, local(): lax.all_to_all(predicted.astype(jnp.bfloat16), 'sup', split_axis=0, conca...  6.34 us
  transfers between devices with their start and end apart: 5, of which 4 were waited for; matrix products, arithmetic and copies ran while one was open for 4% of the time, Pallas kernels for 0%

commit v1 on v0

--- a/solution.py
+++ b/solution.py
@@ -79,7 +79,9 @@
     predictions = lax.all_to_all(
         predicted.astype(jnp.bfloat16), "sup", split_axis=0, concat_axis=1, tiled=True
     )
-    hypergrad = lax.all_to_all(hyper_cols, "sup", split_axis=0, concat_axis=1, tiled=True)
+    pieces = jnp.split(hyper_cols, lax.axis_size("sup"), axis=0)
+    received = lax.all_to_all(jnp.stack(pieces), "sup", 0, 0)
+    hypergrad = jnp.concatenate(received, axis=1)
     return (predictions, hypergrad)
 
 

time: 185 us -> 193 us (1.043)
  local copies, waits for them, and re-layouts: 11.3 us -> 21.6 us
  waiting for transfers between devices: 73.6 us -> 67.9 us
  starting transfers between devices: 17.7 us -> 21 us
    unnamed x8 -> x23, local copies, waits for them, and re-layouts: 3.47 us -> 12.6 us
    all_to_all x1, waiting for transfers between devices: 6.34 us -> 0.01 us  [local(): lax.all_to_all(predicted.astype(jnp.bfloat16), 'sup', split_axis=0, conca...]
    all_to_all x1, starting transfers between devices: 3.57 us -> 6.88 us  [local(): received = lax.all_to_all(jnp.stack(pieces), 'sup', 0, 0)]
    another operation x0 -> x18, local copies, waits for them, and re-layouts: none -> 2.13 us  [local(): received = lax.all_to_all(jnp.stack(pieces), 'sup', 0, 0)]
  transfers between devices with their start and end apart: 5 -> 5, of which waited for: 4 -> 3; matrix products, arithmetic and copies ran while one was open for 4% -> 8% of each run, Pallas kernels for 0% -> 0%
where the time goes in v1:
time: 193 us
  waiting for transfers between devices  67.9 us (35%)
  blocking collectives  59.1 us (31%)
  local copies, waits for them, and re-layouts  21.6 us (11%)
  starting transfers between devices  21 us (11%)
  between operations  15.5 us (8%)
  matrix products  5.95 us (3%)
    all_gather x1, waiting for transfers between devices, local(): lax.all_gather(support_feats, 'sup', axis=0, tiled=True)  52.1 us
    all_gather x1, blocking collectives, local(): kernels = lax.all_gather(finished, ('sup', 'cls'), axis=0, tiled=True)  41.4 us
    unnamed x2, blocking collectives  17.7 us
    all_to_all x1, waiting for transfers between devices, local(): received = lax.all_to_all(jnp.stack(pieces), 'sup', 0, 0)  14.5 us
    unnamed x23, local copies, waits for them, and re-layouts  12.6 us
    all_to_all x1, starting transfers between devices, local(): lax.all_to_all(soft_labels, 'sup', split_axis=1, concat_axis=0, tiled=True)  8.34 us
    all_to_all x1, starting transfers between devices, local(): received = lax.all_to_all(jnp.stack(pieces), 'sup', 0, 0)  6.88 us
  transfers between devices with their start and end apart: 5, of which 3 were waited for; matrix products, arithmetic and copies ran while one was open for 8% of the time, Pallas kernels for 0%

profile of v1, /device:TPU:0, one launch (start us, length us, event | category | flops | bytes accessed | tf_op | source)
XLA Modules:
  0.0 192.6 jit_solution(3995284523964927333)
XLA Ops:
  7.2 0.7 all-gather.3.cloned.1.call-update
  7.9 1.7 all_to_all.31
  9.6 1.1 copy.48
  10.7 8.3 %all-to-all-start = ((f32[32,16,168]{2,0,1:T(8,128)}), f32[32,16,168]{2,0,1:T(8,128)S(1)}, u32[]{:S(2)}, u32[]{:S(2)}) async-start(f32[32,16,168]{2,0,1:T(8,128)} %copy.48), calls=%async_computation | async-start | bytes 1048576 | tf_op jit(solution)/shard_map/all_to_all | solution.py:63
  19.1 0.7 convert_element_type.31
  19.8 0.8 dynamic_slice.6
  20.5 1.2 dynamic-slice.5
  22.4 1.2 dynamic-slice
  24.3 0.9 dynamic-update-slice
  25.2 14.8 %all-reduce.1 = s32[128]{0:T(128)S(1)} all-reduce(s32[128]{0:T(128)S(1)} %dynamic-update-slice), channel_id=1, replica_groups=mesh['sup'=16,'cls'=2] {'sup'}, use_global_device_ids=true, to_apply=%add.1 | all-reduce | flops 128 | bytes 1024
  40.1 52.1 %all-gather.3.cloned.1.call-done = bf16[512,4096]{1,0:T(8,128)(2,1)} async-done(((bf16[32,4096]{1,0:T(8,128)(2,1)}), bf16[512,4096]{1,0:T(8,128)(2,1)}) %all-gather.3.cloned.1.call-update) | async-done | bytes 4194320 | tf_op jit(solution)/shard_map/all_gather | solution.py:42
  92.2 3.6 %fusion.4 = f32[40,512]{1,0:T(8,128)S(1)} fusion(bf16[512,4096]{1,0:T(8,128)(2,1)} %all-gather.3.cloned.1.call-done, bf16[32,4096]{1,0:T(8,128)(2,1)S(1)} %copy-done, bf16[8,4096]{1,0:T(8,128)(2,1)} %param.6), kind=kOutput, calls=%fused_computation.18 | convolution fusion | flops 168427520 | bytes 4603904 | tf_op jit(solution)/shard_map/dot_general | solution.py:40
  95.8 2.9 %fusion = f32[24,512]{1,0:T(8,128)S(1)} fusion(f32[40,512]{1,0:T(8,128)S(1)} %fusion.4), kind=kCustom, calls=%all-reduce-scatter | all-reduce-scatter fusion | flops 24577 | bytes 131584
  98.8 2.3 %collective-permute-start = (f32[4,512]{1,0:T(4,128)S(1)}, f32[4,512]{1,0:T(4,128)S(1)}, u32[]{:S(2)}, u32[]{:S(2)}) collective-permute-start(f32[4,512]{1,0:T(4,128)S(1)} %slice.10), channel_id=1, source_target_pairs={{0,1},{2,3},{4,5},{6,7},{8,9},{10,11},{12,13},{14,15},{16,17},{18,... | collective-permute-start | bytes 24584
  101.3 0.5 collective-permute-done
  102.1 41.4 %all-gather = bf16[32,20,512]{2,1,0:T(8,128)(2,1)S(1)} all-gather(bf16[1,20,512]{2,1,0:T(8,128)(2,1)S(1)} %fusion.29), channel_id=1, replica_groups=mesh['sup'=16,'cls'=2] {'sup','cls'}, dimensions={0}, use_global_device_ids=true | all-gather | bytes 675840 | tf_op jit(solution)/shard_map/all_gather | solution.py:59
  143.6 0.4 multiply_reduce_fusion.4
  144.1 0.2 multiply_reduce_fusion.3
  144.3 0.5 fusion.1
  144.8 0.3 fusion.34
  145.1 0.2 fusion.20
  145.3 0.5 multiply_reduce_fusion.1
  145.8 0.2 multiply_reduce_fusion
  146.0 0.5 fusion.2
  146.7 0.3 slice_bitcast_fusion.3
  147.1 0.6 constant_dynamic-update-slice_fusion.15
  148.8 0.8 copy.53
  149.6 3.5 %all-to-all-start.1 = ((bf16[16,8,168]{2,1,0:T(8,128)(2,1)}), bf16[16,8,168]{2,1,0:T(8,128)(2,1)S(1)}, u32[]{:S(2)}, u32[]{:S(2)}) async-start(bf16[16,8,168]{2,1,0:T(8,128)(2,1)} %bitcast.7), calls=%async_computation.1 | async-start | bytes 131072 | tf_op jit(solution)/shard_map/all_to_all | solution.py:79
  153.1 0.6 constant_dynamic-update-slice_fusion.14
  153.7 0.6 constant_dynamic-update-slice_fusion.13
  154.3 0.6 constant_dynamic-update-slice_fusion.12
  154.9 0.6 constant_dynamic-update-slice_fusion.11
  155.5 0.6 constant_dynamic-update-slice_fusion.10
  156.1 0.6 constant_dynamic-update-slice_fusion.9
  156.7 0.6 constant_dynamic-update-slice_fusion.8
  157.3 0.6 constant_dynamic-update-slice_fusion.7
  157.9 0.6 constant_dynamic-update-slice_fusion.6
  158.5 0.6 constant_dynamic-update-slice_fusion.5
  159.1 0.6 constant_dynamic-update-slice_fusion.4
  159.8 0.6 constant_dynamic-update-slice_fusion.3
  160.4 0.6 constant_dynamic-update-slice_fusion.2
  161.0 0.6 constant_dynamic-update-slice_fusion.1
  161.6 0.6 constant_dynamic-update-slice_fusion
  162.2 6.9 %all-to-all-start.2 = ((f32[16,32,168]{2,1,0:T(8,128)}), f32[16,32,168]{2,1,0:T(8,128)S(1)}, u32[]{:S(2)}, u32[]{:S(2)}) async-start(f32[16,32,168]{2,1,0:T(8,128)} %constant_dynamic-update-slice_fusion), calls=%async_computation.2 | async-start | bytes 1048576 | tf_op jit(solution)/shard_map/all_to_all | solution.py:83
  169.1 0.8 all_to_all.38
  169.8 14.5 %all-to-all-done.2 = f32[16,32,168]{2,1,0:T(8,128)S(1)} async-done(((f32[16,32,168]{2,1,0:T(8,128)}), f32[16,32,168]{2,1,0:T(8,128)S(1)}, u32[]{:S(2)}, u32[]{:S(2)}) %all-to-all-start.2) | async-done | bytes 344096 | tf_op jit(solution)/shard_map/all_to_all | solution.py:83
  184.4 0.3 copy.71
  184.7 1.0 reshape.76
  (42 shorter events, 2.3 us)
Async XLA Ops:
  7.2 85.1 %copy-start = (bf16[32,4096]{1,0:T(8,128)(2,1)S(1)}, bf16[32,4096]{1,0:T(8,128)(2,1)}, u32[]{:S(2)}) copy-start(bf16[32,4096]{1,0:T(8,128)(2,1)} %param.5) | copy-start | bytes 786436
  7.2 85.1 %all-gather.3.cloned.1.call-start = ((), (), s32[]{:S(2)}) async-start(), calls=%async_computation.3 | async-start | bytes 4456448 | tf_op jit(solution)/shard_map/all_gather | solution.py:42
  10.7 29.4 %all-to-all-start = ((f32[32,16,168]{2,0,1:T(8,128)}), f32[32,16,168]{2,0,1:T(8,128)S(1)}, u32[]{:S(2)}, u32[]{:S(2)}) async-start(f32[32,16,168]{2,0,1:T(8,128)} %copy.48), calls=%async_computation | async-start | bytes 1048576 | tf_op jit(solution)/shard_map/all_to_all | solution.py:63
  98.8 3.1 %collective-permute-start = (f32[4,512]{1,0:T(4,128)S(1)}, f32[4,512]{1,0:T(4,128)S(1)}, u32[]{:S(2)}, u32[]{:S(2)}) collective-permute-start(f32[4,512]{1,0:T(4,128)S(1)} %slice.10), channel_id=1, source_target_pairs={{0,1},{2,3},{4,5},{6,7},{8,9},{10,11},{12,13},{14,15},{16,17},{18,... | collective-permute-start | bytes 24584
  149.6 12.6 %all-to-all-start.1 = ((bf16[16,8,168]{2,1,0:T(8,128)(2,1)}), bf16[16,8,168]{2,1,0:T(8,128)(2,1)S(1)}, u32[]{:S(2)}, u32[]{:S(2)}) async-start(bf16[16,8,168]{2,1,0:T(8,128)(2,1)} %bitcast.7), calls=%async_computation.1 | async-start | bytes 131072 | tf_op jit(solution)/shard_map/all_to_all | solution.py:79
  162.2 22.2 %all-to-all-start.2 = ((f32[16,32,168]{2,1,0:T(8,128)}), f32[16,32,168]{2,1,0:T(8,128)S(1)}, u32[]{:S(2)}, u32[]{:S(2)}) async-start(f32[16,32,168]{2,1,0:T(8,128)} %constant_dynamic-update-slice_fusion), calls=%async_computation.2 | async-start | bytes 1048576 | tf_op jit(solution)/shard_map/all_to_all | solution.py:83
Sparse Core Ops, SparseCore 0:
  10.7 81.4 all-gather.2
